TPU v7x, 256 devices: a whole 4x4x8 slice. The times are simulated.
256 devices in a mesh: row: 8 (over z), col: 32 (over y, x, core).
Axes of the slice: x: 4, y: 4, z: 8, core: 2. Of those that a mesh axis runs over, the one named last changes fastest.
Arguments:
- ancestor_inverse: bfloat16 [24576, 24576], P('row', 'col'), may hold values from -6 to 6
- factor_slots: bfloat16 [3, 16384, 512], P(None, ('row', 'col')), may hold values from -0.25 to 0.25
- slot_tiles: int32 [3, 64], replicated, may hold values from -1 to 95, as said below
- parent_factor: bfloat16 [2, 512, 512], replicated, may hold values from -0.25 to 0.25
- diag_inverse: float32 [3, 512, 512], replicated, may hold values from -6 to 6
Outputs:
- inverse_panels: bfloat16 [3, 24576, 512], P(None, ('row', 'col'))
- diag_blocks: float32 [3, 512, 512], replicated
- parent_blocks: float32 [2, 512, 512], replicated
Inputs may be any that keep to these rules, and one draw needn't show every extreme that they name: `slot_tiles`: entries b * 2 to b * 2 + 1 of a supernode's row are the slots of column block b: each is -1 (empty) or names a tile from b * 3 to b * 3 + 2, no tile twice; in each supernode some block has all its slots filled. `factor_slots`: rows of an empty slot are not part of the factor.
All inputs are finite; a program needn't handle non-finite values.
Results may differ from a plain program's by a relative error of at most 0.00075.
Values may be sent and summed in bfloat16 or wider, within the bound.
No kernel may reach another device: no remote copies, remote signals or barrier semaphores. Data moves between devices by JAX's collectives and lax.ppermute only.
A program may use at most 128 MiB of HBM per device.

v0:
```python
import jax
import jax.numpy as jnp
from jax import lax
from jax.sharding import PartitionSpec as P

TILE = 256
CAP = 2
exact_mode = lax.Precision.HIGHEST


def spread(shard, axis, root):
    mine = lax.axis_index(axis) == root
    return lax.psum(jnp.where(mine, shard, jnp.zeros_like(shard)), axis)


def padded_block(slot_data, slot_ids, block_index, tiles_per_block, tile_rows):
    local_tile = slot_ids - block_index * tiles_per_block
    pieces = []
    for tile_index in range(tiles_per_block):
        chosen = jnp.zeros((tile_rows, slot_data.shape[1]), slot_data.dtype)
        for member in range(slot_ids.shape[0]):
            chosen = jnp.where(
                local_tile[member] == tile_index,
                slot_data[member * tile_rows : (member + 1) * tile_rows],
                chosen,
            )
        pieces.append(chosen)
    return jnp.concatenate(pieces, axis=0)


def chosen_columns(inverse_block, slot_ids, block_index, tiles_per_block, tile_rows):
    local_tile = jnp.clip(slot_ids - block_index * tiles_per_block, 0, tiles_per_block - 1)
    pieces = [
        lax.dynamic_slice_in_dim(inverse_block, local_tile[member] * tile_rows, tile_rows, 1)
        for member in range(slot_ids.shape[0])
    ]
    return jnp.concatenate(pieces, axis=1)


def masked_rows(slot_data, slot_ids, tile_rows):
    live_rows = jnp.repeat(slot_ids >= 0, tile_rows)
    return jnp.where(live_rows[:, None], slot_data, jnp.zeros_like(slot_data))


def on_device(ancestor_inverse, factor_slots, slot_tiles, parent_factor, diag_inverse):
    row_count = lax.axis_size("row")
    col_count = lax.axis_size("col")
    row_index = lax.axis_index("row")
    col_index = lax.axis_index("col")
    block_rows, block_cols = ancestor_inverse.shape
    tile_rows = TILE
    tiles_per_block = block_cols // tile_rows
    node_count = factor_slots.shape[0]
    slot_count = CAP
    slot_rows = slot_count * tile_rows
    groups_per_row = col_count // row_count
    panel_rows = block_rows // col_count
    own_block = row_index * groups_per_row + col_index // row_count
    own_offset = col_index % row_count * panel_rows
    slot_start = col_index % groups_per_row * slot_rows
    owner_row = col_index // groups_per_row

    def finish(node, first_total, second_total, prev_diag):
        if node == 0:
            return (diag_inverse[0] - first_total, None)
        parent_link = parent_factor[node - 1].astype(jnp.float32)
        upper = -(second_total + jnp.dot(prev_diag, parent_link, precision=exact_mode))
        diagonal = (
            diag_inverse[node] - first_total - jnp.dot(parent_link.T, upper, precision=exact_mode)
        )
        return (diagonal, upper)

    def node_sums(node, first_part, second_part):
        if node == 0:
            return (lax.psum(first_part, ("row", "col")), None)
        return lax.psum((first_part, second_part), ("row", "col"))

    panels = []
    diagonals = []
    parents = []
    previous = None
    prev_diag = None
    for node in range(node_count):
        row_slots = lax.all_gather(factor_slots[node], "col", axis=0, tiled=True)
        mine = lax.dynamic_slice_in_dim(row_slots, slot_start, slot_rows, 0)
        col_slots = spread(mine, "row", owner_row)
        tiles_node = slot_tiles[node]
        col_ids = lax.dynamic_slice_in_dim(tiles_node, col_index * slot_count, slot_count)
        prepare_columns = chosen_columns(
            ancestor_inverse, col_ids, col_index, tiles_per_block, tile_rows
        )
        prepare_weights = masked_rows(col_slots, col_ids, tile_rows)
        own_ids = lax.dynamic_slice_in_dim(tiles_node, own_block * slot_count, slot_count)
        own_slots = lax.dynamic_slice_in_dim(
            row_slots, col_index // row_count * slot_rows, slot_rows, 0
        )
        own_padded = padded_block(own_slots, own_ids, own_block, tiles_per_block, tile_rows)
        own_rows = lax.dynamic_slice_in_dim(own_padded, own_offset, panel_rows, 0)
        row_padded = None
        columns, weights, own_rows, row_padded = (
            prepare_columns,
            prepare_weights,
            own_rows.astype(jnp.float32),
            row_padded,
        )
        second_part = None
        if node > 0:
            second_part = jnp.dot(previous.T, own_rows, precision=exact_mode)
        summed = lax.psum_scatter(
            jnp.dot(columns, weights, preferred_element_type=jnp.float32),
            "col",
            scatter_dimension=0,
            tiled=True,
        )
        column = -summed
        if node > 0:
            advance_parent_link = parent_factor[node - 1].astype(jnp.float32)
            column = column - jnp.dot(previous, advance_parent_link, precision=exact_mode)
        first_part = jnp.dot(own_rows.T, column, precision=exact_mode)
        first_total, second_total = node_sums(node, first_part, second_part)
        diagonal, upper = finish(node, first_total, second_total, prev_diag)
        panels.append(column.astype(jnp.bfloat16))
        diagonals.append(diagonal)
        if node > 0:
            parents.append(upper)
        previous = column
        prev_diag = diagonal
    return (jnp.stack(panels), jnp.stack(diagonals), jnp.stack(parents))


def solution(mesh):
    placed = (P("row", "col"), P(None, ("row", "col"), None), P(), P(), P())
    return jax.shard_map(
        on_device,
        mesh=mesh,
        in_specs=placed,
        out_specs=(P(None, ("row", "col"), None), P(), P()),
        check_vma=False,
    )
```

profile of v0, /device:TPU:8, one launch (start us, length us, event | category | flops | bytes accessed | tf_op | source)
XLA Modules:
  0.0 841.9 jit_solution(13287973406344088835)
XLA Ops:
  7.2 0.0 all-gather.9.cloned.1.call-start
  7.2 1.6 fusion.71
  8.8 0.0 all-gather.9.cloned.1.call-update
  8.8 0.0 all-gather.7.cloned.1.call-start
  8.9 0.7 all-gather.7.cloned.1.call-update
  9.6 0.0 all-gather.11.cloned.1.call-start
  9.6 0.7 all-gather.11.cloned.1.call-update
  10.3 0.0 all-reduce.7.cloned.1.call-start
  10.4 51.9 %all-gather.9.cloned.1.call-done = bf16[1,2048,512]{2,1,0:T(8,128)(2,1)} async-done(((bf16[1,64,512]{2,1,0:T(8,128)(2,1)}), bf16[1,2048,512]{2,1,0:T(8,128)(2,1)}) %all-gather.9.cloned.1.call-update) | async-done | bytes 2097168 | tf_op jit(solution)/shard_map/all_gather | solution.py:84
  62.3 1.9 select_bitcast_fusion.1
  64.2 49.2 %all-gather.7.cloned.1.call-done = bf16[1,2048,512]{2,1,0:T(8,128)(2,1)} async-done(((bf16[1,64,512]{2,1,0:T(8,128)(2,1)}), bf16[1,2048,512]{2,1,0:T(8,128)(2,1)}) %all-gather.7.cloned.1.call-update) | async-done | bytes 2097168 | tf_op jit(solution)/shard_map/all_gather | solution.py:84
  113.4 1.9 select_bitcast_fusion.2
  115.3 49.2 %all-gather.11.cloned.1.call-done = bf16[1,2048,512]{2,1,0:T(8,128)(2,1)} async-done(((bf16[1,64,512]{2,1,0:T(8,128)(2,1)}), bf16[1,2048,512]{2,1,0:T(8,128)(2,1)}) %all-gather.11.cloned.1.call-update) | async-done | bytes 2097168 | tf_op jit(solution)/shard_map/all_gather | solution.py:84
  164.5 1.9 select_bitcast_fusion
  166.4 0.0 all-reduce.7.cloned.1.call-update
  166.5 0.0 reduce-scatter.6.cloned.1.call-start
  166.6 0.1 fusion.56
  166.6 0.6 fusion.75
  168.5 0.1 fusion.54
  168.6 0.6 fusion.77
  170.4 0.7 fusion.78
  172.4 0.1 compare_bitcast_fusion
  172.5 0.1 broadcast_in_dim.36
  172.6 6.8 constant_dynamic-slice_fusion.4
  179.5 66.0 %all-reduce.7.cloned.1.call-done = (bf16[512,512]{1,0:T(8,128)(2,1)}, bf16[512,512]{1,0:T(8,128)(2,1)}, bf16[512,512]{1,0:T(8,128)(2,1)}) async-done(((bf16[512,512]{1,0:T(8,128)(2,1)}, bf16[512,512]{1,0:T(8,128)(2,1)}, bf16[512,512]{1,0:T(8,128)(2,1)}), (bf16[512,512]{1,0:T(8,128)(2,1)}, bf16[512,512]{1,0:T(8,128)(2,1)}, bf16[512,512]{1,0:T(8,128)(2,1)})) %all-reduce.7.cloned.1.call-update) | async-done | bytes 1572880 | tf_op jit(solution)/shard_map/psum | solution.py:13
  245.4 6.5 fusion.4
  251.9 0.0 reduce-scatter.6.cloned.1.call-update
  252.0 0.0 reduce-scatter.4.cloned.1.call-start
  252.0 0.1 compare_bitcast_fusion.2
  252.1 0.1 broadcast_in_dim.33
  252.2 6.5 fusion
  258.7 0.0 reduce-scatter.4.cloned.1.call-update
  258.7 0.0 reduce-scatter.8.cloned.1.call-start
  258.7 0.1 broadcast_in_dim.39
  258.8 5.5 fusion.8
  264.3 0.0 reduce-scatter.8.cloned.1.call-update
  264.4 0.2 all-reduce.5.cloned.1.call-start
  264.6 0.6 fusion.73
  272.8 0.6 fusion.74
  277.3 1.2 select_bitcast_fusion.8
  278.5 2.0 select_bitcast_fusion.10
  280.5 1.2 select_bitcast_fusion.5
  281.7 63.3 %reduce-scatter.6.cloned.1.call-done = f32[96,512]{1,0:T(8,128)} async-done(((f32[3072,512]{1,0:T(8,128)}), f32[96,512]{1,0:T(8,128)}) %reduce-scatter.6.cloned.1.call-update) | async-done | bytes 196624 | tf_op jit(solution)/shard_map/reduce_scatter | solution.py:109
  345.0 97.1 %reduce-scatter.4.cloned.1.call-done = f32[96,512]{1,0:T(8,128)} async-done(((f32[3072,512]{1,0:T(8,128)}), f32[96,512]{1,0:T(8,128)}) %reduce-scatter.4.cloned.1.call-update) | async-done | bytes 196624 | tf_op jit(solution)/shard_map/reduce_scatter | solution.py:109
  442.1 1.4 convolution_subtract_fusion.1
  443.5 1.7 fusion.69
  445.2 94.2 %reduce-scatter.8.cloned.1.call-done = f32[96,512]{1,0:T(8,128)} async-done(((f32[3072,512]{1,0:T(8,128)}), f32[96,512]{1,0:T(8,128)}) %reduce-scatter.8.cloned.1.call-update) | async-done | bytes 196624 | tf_op jit(solution)/shard_map/reduce_scatter | solution.py:109
  539.4 1.3 convolution_subtract_fusion
  540.7 1.7 fusion.67
  542.5 1.7 fusion.64
  544.2 1.7 fusion.39
  545.8 1.8 fusion.41
  547.7 0.0 all-reduce.5.cloned.1.call-update
  547.8 0.7 pad_maximum_fusion.2
  548.5 274.5 %all-reduce.5.cloned.1.call-done = (f32[512,512]{1,0:T(8,128)}, f32[512,512]{1,0:T(8,128)}, f32[512,512]{1,0:T(8,128)}, f32[512,512]{1,0:T(8,128)}, f32[512,512]{1,0:T(8,128)}) async-done(((f32[512,512]{1,0:T(8,128)}, f32[512,512]{1,0:T(8,128)}, f32[512,512]{1,0:T(8,128)}, f32[512,512]{1,0:T(8,128)}, f32[512,512]{1,0:T(8,128)}), (f32[512,512]{1,0:T(8,128)}, f32[512,512]{1,0:T(8,128)}, f32[512,512]{1,0:T(8,128)}, ...) | async-done | bytes 5242896 | tf_op jit(solution)/shard_map/psum | solution.py:76
  823.1 1.9 fusion.29
  825.0 0.6 copy-done.1
  825.6 2.6 fusion.13
  828.2 1.1 fusion.16
  829.3 0.1 copy-done.3
  829.4 1.0 fusion.12
  830.4 1.1 fusion.15
  831.5 1.5 pad_maximum_fusion.1
  833.0 2.0 pad_maximum_fusion
  (23 shorter events, 0.2 us)
Async XLA Ops:
  7.2 159.4 %copy-start.8 = (s32[3,64]{1,0:T(4,128)S(1)}, s32[3,64]{1,0:T(4,128)}, u32[]{:S(2)}) copy-start(s32[3,64]{1,0:T(4,128)} %param.7) | copy-start | bytes 2308
  7.2 55.1 %all-gather.9.cloned.1.call-start = ((), (), s32[]{:S(2)}) async-start(), calls=%async_computation.7 | async-start | bytes 2162688 | tf_op jit(solution)/shard_map/all_gather | solution.py:84
  8.8 104.6 %all-gather.7.cloned.1.call-start = ((), (), s32[]{:S(2)}) async-start(), calls=%async_computation.6 | async-start | bytes 2162688 | tf_op jit(solution)/shard_map/all_gather | solution.py:84
  9.6 154.9 %all-gather.11.cloned.1.call-start = ((), (), s32[]{:S(2)}) async-start(), calls=%async_computation.8 | async-start | bytes 2162688 | tf_op jit(solution)/shard_map/all_gather | solution.py:84
  10.3 235.1 %all-reduce.7.cloned.1.call-start = ((), (), s32[]{:S(2)}) async-start(), calls=%async_computation.10 | async-start | bytes 3145728 | tf_op jit(solution)/shard_map/psum | solution.py:13
  166.5 178.5 %reduce-scatter.6.cloned.1.call-start = ((), (), s32[]{:S(2)}) async-start(), calls=%async_computation.4 | async-start | bytes 6488064 | tf_op jit(solution)/shard_map/reduce_scatter | solution.py:109
  252.0 190.1 %reduce-scatter.4.cloned.1.call-start = ((), (), s32[]{:S(2)}) async-start(), calls=%async_computation.3 | async-start | bytes 6488064 | tf_op jit(solution)/shard_map/reduce_scatter | solution.py:109
  258.7 280.7 %reduce-scatter.8.cloned.1.call-start = ((), (), s32[]{:S(2)}) async-start(), calls=%async_computation.5 | async-start | bytes 6488064 | tf_op jit(solution)/shard_map/reduce_scatter | solution.py:109
  264.4 177.7 %copy-start = (bf16[2,512,512]{2,1,0:T(8,128)(2,1)S(1)}, bf16[2,512,512]{2,1,0:T(8,128)(2,1)}, u32[]{:S(2)}) copy-start(bf16[2,512,512]{2,1,0:T(8,128)(2,1)} %param.8) | copy-start | bytes 3145732
  264.4 558.7 %all-reduce.5.cloned.1.call-start = ((), (), s32[]{:S(2)}) async-start(), calls=%async_computation.9 | async-start | bytes 10485760 | tf_op jit(solution)/shard_map/psum | solution.py:76
  443.5 100.7 %copy-start.2 = (f32[96,512]{1,0:T(8,128)S(1)}, f32[96,512]{1,0:T(8,128)}, u32[]{:S(2)}) copy-start(f32[96,512]{1,0:T(8,128)} %reduce-scatter.4.cloned.1.call-done) | copy-start | bytes 589828
  540.7 5.1 copy-start.4
  540.7 5.1 copy-start.5
  823.0 2.5 copy-start.1
  825.0 3.2 copy-start.7
  828.2 1.2 copy-start.3
  828.2 2.2 copy-start.6
Sparse Core Ops, SparseCore 0:
  11.1 51.0 all-gather.8
  65.4 47.9 all-gather.6
  116.5 47.9 all-gather.10
  167.0 78.4 all-reduce.6
  252.1 92.8 reduce-scatter.5
  348.9 93.1 reduce-scatter.3
  446.1 93.2 reduce-scatter.7
  547.8 275.1 all-reduce.4
where the time goes:
time: 843 us; the launch traced here: 842 us
  waiting for transfers between devices  747 us (89%)
  matrix products  35.6 us (4%)
  between operations  29.7 us (4%)
  other arithmetic  16.8 us (2%)
  local copies, waits for them, and re-layouts  12.5 us (1%)
    psum x1, waiting for transfers between devices, node_sums(): return lax.psum((first_part, second_part), ('row', 'col'))  275 us
    reduce_scatter x3, waiting for transfers between devices, on_device(): lax.psum_scatter(jnp.dot(columns, weights, preferred_element_type=jnp.flo...  255 us
    all_gather x3, waiting for transfers between devices, on_device(): row_slots = lax.all_gather(factor_slots[node], 'col', axis=0, tiled=True)  150 us
    psum x1, waiting for transfers between devices, spread(): return lax.psum(jnp.where(mine, shard, jnp.zeros_like(shard)), axis)  66 us
    dot_general x3, matrix products, on_device(): jnp.dot(columns, weights, preferred_element_type=jnp.float32)  18.5 us
  transfers between devices with their start and end apart: 8, of which 8 were waited for; matrix products, arithmetic and copies ran while one was open for 4% of the time, Pallas kernels for 0%

commit v1 on v0

--- a/solution.py
+++ b/solution.py
@@ -73,7 +73,7 @@
     def node_sums(node, first_part, second_part):
         if node == 0:
             return (lax.psum(first_part, ("row", "col")), None)
-        return lax.psum((first_part, second_part), ("row", "col"))
+        return lax.psum(lax.psum((first_part, second_part), "col"), "row")
 
     panels = []
     diagonals = []

time: 843 us -> 1060 us (1.26)
  waiting for transfers between devices: 747 us -> 965 us
    psum x1 -> x3, waiting for transfers between devices: 275 us -> 486 us  [the longest x1 264 us: node_sums(): return (lax.psum(first_part, ('row', 'col')), None)]
  transfers between devices with their start and end apart: 8 -> 10, of which waited for: 8 -> 10; matrix products, arithmetic and copies ran while one was open for 4% -> 4% of each run, Pallas kernels for 0% -> 0%
where the time goes in v1:
time: 1060 us
  waiting for transfers between devices  965 us (91%)
  matrix products  35.8 us (3%)
  between operations  29.5 us (3%)
  other arithmetic  15.8 us (1%)
  local copies, waits for them, and re-layouts  11.8 us (1%)
    psum x1, waiting for transfers between devices, node_sums(): return (lax.psum(first_part, ('row', 'col')), None)  264 us
    reduce_scatter x3, waiting for transfers between devices, on_device(): lax.psum_scatter(jnp.dot(columns, weights, preferred_element_type=jnp.flo...  261 us
    psum x2, waiting for transfers between devices, node_sums(): return lax.psum(lax.psum((first_part, second_part), 'col'), 'row')  222 us
    all_gather x3, waiting for transfers between devices, on_device(): row_slots = lax.all_gather(factor_slots[node], 'col', axis=0, tiled=True)  150 us
    psum x1, waiting for transfers between devices, spread(): return lax.psum(jnp.where(mine, shard, jnp.zeros_like(shard)), axis)  66 us
  transfers between devices with their start and end apart: 10, of which 10 were waited for; matrix products, arithmetic and copies ran while one was open for 4% of the time, Pallas kernels for 0%

profile of v1, /device:TPU:8, one launch (start us, length us, event | category | flops | bytes accessed | tf_op | source)
XLA Modules:
  0.0 1058.6 jit_solution(10996331505995891116)
XLA Ops:
  7.2 0.0 all-gather.9.cloned.1.call-start
  7.2 1.6 fusion.71
  8.8 0.0 all-gather.9.cloned.1.call-update
  8.8 0.0 all-gather.7.cloned.1.call-start
  8.9 0.7 all-gather.7.cloned.1.call-update
  9.6 0.0 all-gather.11.cloned.1.call-start
  9.6 0.7 all-gather.11.cloned.1.call-update
  10.3 0.0 all-reduce.14.cloned.1.call-start
  10.4 51.9 %all-gather.9.cloned.1.call-done = bf16[1,2048,512]{2,1,0:T(8,128)(2,1)} async-done(((bf16[1,64,512]{2,1,0:T(8,128)(2,1)}), bf16[1,2048,512]{2,1,0:T(8,128)(2,1)}) %all-gather.9.cloned.1.call-update) | async-done | bytes 2097168 | tf_op jit(solution)/shard_map/all_gather | solution.py:84
  62.3 1.9 select_bitcast_fusion.1
  64.2 49.2 %all-gather.7.cloned.1.call-done = bf16[1,2048,512]{2,1,0:T(8,128)(2,1)} async-done(((bf16[1,64,512]{2,1,0:T(8,128)(2,1)}), bf16[1,2048,512]{2,1,0:T(8,128)(2,1)}) %all-gather.7.cloned.1.call-update) | async-done | bytes 2097168 | tf_op jit(solution)/shard_map/all_gather | solution.py:84
  113.4 1.9 select_bitcast_fusion.2
  115.3 49.2 %all-gather.11.cloned.1.call-done = bf16[1,2048,512]{2,1,0:T(8,128)(2,1)} async-done(((bf16[1,64,512]{2,1,0:T(8,128)(2,1)}), bf16[1,2048,512]{2,1,0:T(8,128)(2,1)}) %all-gather.11.cloned.1.call-update) | async-done | bytes 2097168 | tf_op jit(solution)/shard_map/all_gather | solution.py:84
  164.5 1.9 select_bitcast_fusion
  166.4 0.0 all-reduce.14.cloned.1.call-update
  166.5 0.0 reduce-scatter.6.cloned.1.call-start
  166.6 0.1 fusion.56
  166.6 0.6 fusion.75
  168.6 0.1 fusion.54
  168.7 0.6 fusion.77
  170.6 0.6 fusion.78
  172.4 0.1 compare_bitcast_fusion
  172.5 0.1 broadcast_in_dim.36
  172.6 6.8 constant_dynamic-slice_fusion.4
  179.4 66.0 %all-reduce.14.cloned.1.call-done = (bf16[512,512]{1,0:T(8,128)(2,1)}, bf16[512,512]{1,0:T(8,128)(2,1)}, bf16[512,512]{1,0:T(8,128)(2,1)}) async-done(((bf16[512,512]{1,0:T(8,128)(2,1)}, bf16[512,512]{1,0:T(8,128)(2,1)}, bf16[512,512]{1,0:T(8,128)(2,1)}), (bf16[512,512]{1,0:T(8,128)(2,1)}, bf16[512,512]{1,0:T(8,128)(2,1)}, bf16[512,512]{1,0:T(8,128)(2,1)})) %all-reduce.14.cloned.1.call-update) | async-done | bytes 1572880 | tf_op jit(solution)/shard_map/psum | solution.py:13
  245.4 6.5 fusion.4
  251.9 0.0 reduce-scatter.6.cloned.1.call-update
  252.0 0.0 reduce-scatter.4.cloned.1.call-start
  252.0 0.1 compare_bitcast_fusion.2
  252.1 0.1 broadcast_in_dim.33
  252.2 6.5 fusion
  258.7 0.0 reduce-scatter.8.cloned.1.call-start
  258.7 0.1 broadcast_in_dim.39
  258.8 5.5 fusion.8
  264.4 0.0 all-reduce.10.cloned.1.call-start
  268.3 0.6 fusion.74
  272.5 1.2 select_bitcast_fusion.8
  273.7 1.2 select_bitcast_fusion.5
  274.9 70.0 %reduce-scatter.6.cloned.1.call-done = f32[96,512]{1,0:T(8,128)} async-done(((f32[3072,512]{1,0:T(8,128)}), f32[96,512]{1,0:T(8,128)}) %reduce-scatter.6.cloned.1.call-update) | async-done | bytes 196624 | tf_op jit(solution)/shard_map/reduce_scatter | solution.py:109
  345.0 97.1 %reduce-scatter.4.cloned.1.call-done = f32[96,512]{1,0:T(8,128)} async-done(((f32[3072,512]{1,0:T(8,128)}), f32[96,512]{1,0:T(8,128)}) %reduce-scatter.4.cloned.1.call-update) | async-done | bytes 196624 | tf_op jit(solution)/shard_map/reduce_scatter | solution.py:109
  442.1 1.4 convolution_subtract_fusion.1
  443.5 1.7 fusion.69
  445.2 94.2 %reduce-scatter.8.cloned.1.call-done = f32[96,512]{1,0:T(8,128)} async-done(((f32[3072,512]{1,0:T(8,128)}), f32[96,512]{1,0:T(8,128)}) %reduce-scatter.8.cloned.1.call-update) | async-done | bytes 196624 | tf_op jit(solution)/shard_map/reduce_scatter | solution.py:109
  539.4 1.3 convolution_subtract_fusion
  540.7 1.8 fusion.67
  542.5 1.8 fusion.64
  544.2 1.7 fusion.39
  545.9 0.0 all-reduce.8.cloned.1.call-start
  546.0 0.6 fusion.73
  550.4 1.2 select_bitcast_fusion.10
  551.6 1.7 fusion.41
  553.3 0.2 all-reduce.12.cloned.1.call-start
  553.6 113.2 %all-reduce.10.cloned.1.call-done = (f32[512,512]{1,0:T(8,128)}, f32[512,512]{1,0:T(8,128)}, f32[512,512]{1,0:T(8,128)}, f32[512,512]{1,0:T(8,128)}) async-done(((f32[512,512]{1,0:T(8,128)}, f32[512,512]{1,0:T(8,128)}, f32[512,512]{1,0:T(8,128)}, f32[512,512]{1,0:T(8,128)}), (f32[512,512]{1,0:T(8,128)}, f32[512,512]{1,0:T(8,128)}, f32[512,512]{1,0:T(8,128)}, ...) | async-done | bytes 4194320 | tf_op jit(solution)/shard_map/psum | solution.py:76
  666.9 0.7 pad_maximum_fusion.2
  667.6 264.1 %all-reduce.8.cloned.1.call-done = f32[512,512]{1,0:T(8,128)} async-done(((f32[512,512]{1,0:T(8,128)}), f32[512,512]{1,0:T(8,128)}) %all-reduce.8.cloned.1.call-update) | async-done | bytes 1048592 | tf_op jit(solution)/shard_map/psum | solution.py:75
  931.7 1.8 fusion.29
  933.6 108.5 %all-reduce.12.cloned.1.call-done = (f32[512,512]{1,0:T(8,128)}, f32[512,512]{1,0:T(8,128)}, f32[512,512]{1,0:T(8,128)}, f32[512,512]{1,0:T(8,128)}) async-done(((f32[512,512]{1,0:T(8,128)}, f32[512,512]{1,0:T(8,128)}, f32[512,512]{1,0:T(8,128)}, f32[512,512]{1,0:T(8,128)}), (f32[512,512]{1,0:T(8,128)}, f32[512,512]{1,0:T(8,128)}, f32[512,512]{1,0:T(8,128)}, ...) | async-done | bytes 4194320 | tf_op jit(solution)/shard_map/psum | solution.py:76
  1042.1 2.7 fusion.13
  1044.8 0.1 copy-done.6
  1044.9 1.2 fusion.16
  1046.1 1.0 fusion.12
  1047.1 1.2 fusion.15
  1048.3 1.5 pad_maximum_fusion.1
  1049.8 2.0 pad_maximum_fusion
  (27 shorter events, 0.2 us)
Async XLA Ops:
  7.2 159.4 %copy-start.7 = (s32[3,64]{1,0:T(4,128)S(1)}, s32[3,64]{1,0:T(4,128)}, u32[]{:S(2)}) copy-start(s32[3,64]{1,0:T(4,128)} %param.7) | copy-start | bytes 2308
  7.2 55.1 %all-gather.9.cloned.1.call-start = ((), (), s32[]{:S(2)}) async-start(), calls=%async_computation.8 | async-start | bytes 2162688 | tf_op jit(solution)/shard_map/all_gather | solution.py:84
  8.8 104.6 %all-gather.7.cloned.1.call-start = ((), (), s32[]{:S(2)}) async-start(), calls=%async_computation.7 | async-start | bytes 2162688 | tf_op jit(solution)/shard_map/all_gather | solution.py:84
  9.6 154.9 %all-gather.11.cloned.1.call-start = ((), (), s32[]{:S(2)}) async-start(), calls=%async_computation.9 | async-start | bytes 2162688 | tf_op jit(solution)/shard_map/all_gather | solution.py:84
  10.3 235.1 %all-reduce.14.cloned.1.call-start = ((), (), s32[]{:S(2)}) async-start(), calls=%async_computation.12 | async-start | bytes 3145728 | tf_op jit(solution)/shard_map/psum | solution.py:13
  166.5 178.5 %reduce-scatter.6.cloned.1.call-start = ((), (), s32[]{:S(2)}) async-start(), calls=%async_computation.4 | async-start | bytes 6488064 | tf_op jit(solution)/shard_map/reduce_scatter | solution.py:109
  252.0 190.1 %reduce-scatter.4.cloned.1.call-start = ((), (), s32[]{:S(2)}) async-start(), calls=%async_computation.3 | async-start | bytes 6488064 | tf_op jit(solution)/shard_map/reduce_scatter | solution.py:109
  258.7 280.7 %reduce-scatter.8.cloned.1.call-start = ((), (), s32[]{:S(2)}) async-start(), calls=%async_computation.5 | async-start | bytes 6488064 | tf_op jit(solution)/shard_map/reduce_scatter | solution.py:109
  264.3 177.8 %copy-start = (bf16[2,512,512]{2,1,0:T(8,128)(2,1)S(1)}, bf16[2,512,512]{2,1,0:T(8,128)(2,1)}, u32[]{:S(2)}) copy-start(bf16[2,512,512]{2,1,0:T(8,128)(2,1)} %param.8) | copy-start | bytes 3145732
  264.4 402.4 %all-reduce.10.cloned.1.call-start = ((), (), s32[]{:S(2)}) async-start(), calls=%async_computation.10 | async-start | bytes 8388608 | tf_op jit(solution)/shard_map/psum | solution.py:76
  443.5 100.7 %copy-start.3 = (f32[96,512]{1,0:T(8,128)S(1)}, f32[96,512]{1,0:T(8,128)}, u32[]{:S(2)}) copy-start(f32[96,512]{1,0:T(8,128)} %reduce-scatter.4.cloned.1.call-done) | copy-start | bytes 589828
  545.9 385.8 %all-reduce.8.cloned.1.call-start = ((), (), s32[]{:S(2)}) async-start(), calls=%async_computation.6 | async-start | bytes 2097152 | tf_op jit(solution)/shard_map/psum | solution.py:75
  553.3 488.7 %all-reduce.12.cloned.1.call-start = ((), (), s32[]{:S(2)}) async-start(), calls=%async_computation.11 | async-start | bytes 8388608 | tf_op jit(solution)/shard_map/psum | solution.py:76
  931.7 110.4 %copy-start.2 = (f32[512,512]{1,0:T(8,128)S(1)}, f32[512,512]{1,0:T(8,128)}, u32[]{:S(2)}) copy-start(f32[512,512]{1,0:T(8,128)} %all-reduce.8.cloned.1.call-done) | copy-start | bytes 3145732
  1042.1 2.7 copy-start.1
  1042.1 2.8 copy-start.6
  1044.8 1.2 copy-start.4
  1044.9 2.2 copy-start.5
Sparse Core Ops, SparseCore 0:
  11.1 51.0 all-gather.8
  65.4 47.9 all-gather.6
  116.5 47.9 all-gather.10
  167.0 78.4 all-reduce.13
  252.1 92.8 reduce-scatter.5
  348.9 93.1 reduce-scatter.3
  446.1 93.2 reduce-scatter.7
  546.1 120.6 all-reduce.9
  672.2 259.4 all-reduce.7
  934.2 107.8 all-reduce.11
